TPU v7x, 32 devices: a whole 2x2x4 slice. The times are simulated.
32 devices in a mesh: row: 8 (over z, x), col: 4 (over y, core).
Axes of the slice: x: 2, y: 2, z: 4, core: 2. Of those that a mesh axis runs over, the one named last changes fastest.
Arguments:
- panel: float32 [2560, 256], P('row', 'col'), may hold values from 0 to 65520, as said below
- trail: float32 [2560, 16384], P('row', 'col'), may hold values from 0 to 65520, as said below
- leaf_pick: int32 [8, 256], P('row'), may hold values from 0 to 319, as said below
- node_pick: int32 [7, 256], replicated, may hold values from 0 to 511, as said below
Outputs:
- schur: float32 [2560, 16384], P('row', 'col')
- multipliers: float32 [2560, 256], P('row')
Inputs may be any that keep to these rules, and one draw needn't show every extreme that they name: `leaf_pick`: each row holds 256 different local row numbers. `node_pick`: each row holds 256 different positions among the node's 2 * 256 candidates. Entries are whole residues; the panel rows of pivot_ids, in that order, form a unit upper-triangular matrix modulo 65521. `trail`: entries are whole residues.
All inputs are finite; a program needn't handle non-finite values.
Results may differ from a plain program's by a relative error of at most 0.0003.
Values sent between devices are 32-bit elements; how exact they have to be, the bound alone decides.
No kernel may reach another device: no remote copies, remote signals or barrier semaphores. Data moves between devices by JAX's collectives and lax.ppermute only.
A program may use at most 128 MiB of HBM per device.

v0:
```python
import jax
import jax.numpy as jnp
from jax import lax
from jax.sharding import PartitionSpec as P

MODULUS = 65521.0


def swapped(block, axis, bit):
    count = lax.axis_size(axis)
    route = []
    for low in range(count):
        high = low | 1 << bit
        if high != low and high < count:
            route += [(low, high), (high, low)]
    return lax.ppermute(block, axis, route)


def residue(values):
    return jnp.mod(values, MODULUS)


def limbs(values):
    upper_limb = jnp.floor(values / 256.0)
    lower_limb = values - 256.0 * upper_limb
    return (upper_limb.astype(jnp.bfloat16), lower_limb.astype(jnp.bfloat16))


def modmul(first_factor, second_factor):
    first_upper, first_lower = limbs(first_factor)
    second_upper, second_lower = limbs(second_factor)
    high_part = residue(jnp.dot(first_upper, second_upper, preferred_element_type=jnp.float32))
    cross_one = residue(jnp.dot(first_upper, second_lower, preferred_element_type=jnp.float32))
    cross_two = residue(jnp.dot(first_lower, second_upper, preferred_element_type=jnp.float32))
    low_part = residue(jnp.dot(first_lower, second_lower, preferred_element_type=jnp.float32))
    middle = residue(cross_one + cross_two)
    return residue(residue(15.0 * high_part) + residue(256.0 * middle) + low_part)


def invert_unit(pivot_block):
    width = pivot_block.shape[0]
    identity = jnp.eye(width, dtype=jnp.float32)
    nilpotent = pivot_block - identity
    inverse = residue(identity - nilpotent + MODULUS)
    power = nilpotent
    for section in range((width - 1).bit_length() - 1):
        power = modmul(power, power)
        inverse = modmul(inverse, residue(identity + power))
    return inverse


def merge_candidates(owned, partner, place, height, devices, node_pick):
    upper_half = place >> height & 1
    node_index = devices - (devices >> height) + (place >> height + 1)
    picked = node_pick[node_index]

    def join(mine_part, their_part):
        lower_first = jnp.concatenate([mine_part, their_part], axis=0)
        upper_first = jnp.concatenate([their_part, mine_part], axis=0)
        stacked = jnp.where(upper_half == 0, lower_first, upper_first)
        return stacked[picked]

    return jax.tree.map(join, owned, partner)


def per_device(panel, trail, leaf_pick, node_pick):
    row_count = panel.shape[0]
    part_width = panel.shape[1]
    place = lax.axis_index("row")
    devices = lax.axis_size("row")
    depth_count = devices.bit_length() - 1
    own_picks = leaf_pick[0]
    held = (panel[own_picks], place * row_count + own_picks)
    for height in range(depth_count):
        partner = swapped((held[0], held[1]), "row", height)
        held = merge_candidates(held, partner, place, height, devices, node_pick)
    block_part, row_ids = held
    owned = (row_ids // row_count == place).astype(jnp.float32)[:, None]
    local_rows = row_ids % row_count
    pivot_trail = lax.psum(trail[local_rows] * owned, "row")
    pivot_block = lax.all_gather(block_part, "col", axis=1, tiled=True)
    inverse = invert_unit(pivot_block)
    first_col = lax.axis_index("col") * part_width
    inverse_rows = lax.dynamic_slice_in_dim(inverse, first_col, part_width, 0)
    factors = residue(lax.psum(modmul(panel, inverse_rows), "col"))
    remainder = residue(trail + (MODULUS - modmul(factors, pivot_trail)))
    return (remainder / MODULUS, factors / MODULUS)


def solution(mesh):
    in_specs = (P("row", "col"), P("row", "col"), P("row", None), P())
    out_specs = (P("row", "col"), P("row", None))
    return jax.shard_map(
        per_device, mesh=mesh, in_specs=in_specs, out_specs=out_specs, check_vma=False
    )
```

profile of v0, /device:TPU:0, one launch (start us, length us, event | category | flops | bytes accessed | tf_op | source)
XLA Modules:
  0.0 318.5 jit_solution(15602679436969307907)
XLA Ops:
  7.2 1.0 copy.8
  9.6 3.0 collective-permute-start
  14.2 2.7 collective-permute-done.3
  16.9 1.9 gather_fusion.4
  18.9 1.6 collective-permute-start.4
  20.5 2.0 collective-permute-done.4
  22.5 1.9 gather_fusion.5
  24.5 2.7 collective-permute-start.5
  27.1 1.9 collective-permute-done.5
  29.0 1.9 gather_fusion.6
  31.8 1.6 collective-permute-start.1
  33.4 4.7 %collective-permute-done.1 = f32[256,64]{1,0:T(8,128)S(1)} collective-permute-done((f32[256,64]{1,0:T(8,128)S(1)}, f32[256,64]{1,0:T(8,128)S(1)}, u32[]{:S(2)}, u32[]{:S(2)}) %collective-permute-start.1) | collective-permute-done | bytes 65568 | tf_op jit(solution)/shard_map/ppermute | solution.py:16
  38.9 2.7 collective-permute-start.2
  41.6 8.2 %gather_fusion.7 = f32[256,4096]{1,0:T(8,128)} fusion(f32[320,4096]{1,0:T(8,128)} %param.5, s32[1024]{0:T(1024)S(1)} %pad_clamp_fusion), kind=kCustom, calls=%fused_computation.7 | custom fusion | bytes 8389632 | tf_op jit(solution)/shard_map/gather | solution.py:80
  50.7 6.2 %all-gather = f32[256,256]{0,1:T(8,128)S(1)} all-gather(f32[256,64]{0,1:T(8,128)S(1)} %copy.9), channel_id=2, replica_groups=mesh['row'=8,'col'=4] {'col'}, dimensions={1}, use_global_device_ids=true | all-gather | bytes 327680 | tf_op jit(solution)/shard_map/all_gather | solution.py:81
  61.0 1.2 add_select_fusion.118
  65.1 1.1 add_select_fusion.101
  69.1 1.1 add_select_fusion.84
  70.2 1.1 add_select_fusion.76
  73.2 1.1 add_select_fusion.67
  77.2 1.1 add_select_fusion.50
  81.2 1.1 add_select_fusion.33
  82.3 1.1 add_select_fusion.24
  86.2 1.9 add_select_fusion.10
  88.1 4.8 %broadcast_multiply_fusion = f32[256,4096]{1,0:T(8,128)} fusion(f32[256,4096]{1,0:T(8,128)} %gather_fusion.7, f32[256]{0:T(256)S(1)} %compare_convert_fusion), kind=kLoop, calls=%fused_computation.37 | loop fusion | flops 1048576 | bytes 8389632 | tf_op jit(solution)/shard_map/mul | solution.py:80
  92.9 25.4 %all-reduce.3.cloned.1.call-done = f32[320,256]{1,0:T(8,128)} async-done(((f32[320,256]{1,0:T(8,128)}), f32[320,256]{1,0:T(8,128)}) %all-reduce.3.cloned.1.call-update) | async-done | bytes 327696 | tf_op jit(solution)/shard_map/psum | solution.py:85
  118.3 1.9 broadcast_multiply_fusion.1
  120.2 158.8 %all-reduce.5.cloned.1.call-done = f32[256,4096]{1,0:T(8,128)} async-done(((f32[256,4096]{1,0:T(8,128)}), f32[256,4096]{1,0:T(8,128)}) %all-reduce.5.cloned.1.call-update) | async-done | bytes 4194320 | tf_op jit(solution)/shard_map/psum | solution.py:80
  279.0 4.5 %convolution_remainder_fusion.3 = f32[320,4096]{1,0:T(8,128)S(1)} fusion(f32[256,4096]{1,0:T(8,128)} %all-reduce.5.cloned.1.call-done, f32[320,256]{1,0:T(8,128)} %all-reduce.3.cloned.1.call-done), kind=kOutput, calls=%fused_computation.20 | convolution fusion | flops 676282368 | bytes 9764864 | tf_op jit(solution)/shard_map/dot_general | solution.py:32
  283.5 2.8 convolution_remainder_fusion.2
  286.3 2.6 convolution_remainder_fusion.1
  288.9 22.2 %fusion.12 = f32[320,4096]{1,0:T(8,128)} fusion(f32[320,4096]{1,0:T(8,128)S(1)} %bitcast.22, f32[320,4096]{1,0:T(8,128)S(1)} %convolution_remainder_fusion.1, f32[320,4096]{1,0:T(8,128)S(1)} %convolution_remainder_fusion.2, f32[320,4096]{1,0:T(8,128)S(1)} %convolution_remainder_fusion.3, f32[256,4096]{1,0:T(8,128)S(1)} %copy-done, f32[320,256]{1,0:T(8,128)S(1)} %copy-done.1), kind=kOutput, calls=%fused_computation.33 | convolution fusion | flops 754565120 | bytes 30736384 | tf_op jit(solution)/shard_map/dot_general | solution.py:35
  (94 shorter events, 25.7 us)
Async XLA Ops:
  7.2 111.2 %all-reduce.3.cloned.1.call-start = ((), (), s32[]{:S(2)}) async-start(), calls=%async_computation | async-start | bytes 655360 | tf_op jit(solution)/shard_map/psum | solution.py:85
  9.6 21.4 %collective-permute-start = (f32[256,64]{1,0:T(8,128)S(1)}, f32[256,64]{1,0:T(8,128)S(1)}, u32[]{:S(2)}, u32[]{:S(2)}) collective-permute-start(f32[256,64]{1,0:T(8,128)S(1)} %gather_fusion), channel_id=1, source_target_pairs={{0,4},{4,0},{8,12},{12,8},{16,20},{20,16},{24,28},{28,24},{1,5},{5... | collective-permute-start | bytes 196616 | tf_op jit(solution)/shard_map/ppermute | solution.py:16
  13.3 3.6 %collective-permute-start.3 = (s32[256]{0:T(256)S(1)}, s32[256]{0:T(256)S(1)}, u32[]{:S(2)}, u32[]{:S(2)}) collective-permute-start(s32[256]{0:T(256)S(1)} %bitcast.29), channel_id=1, source_target_pairs={{0,4},{4,0},{8,12},{12,8},{16,20},{20,16},{24,28},{28,24},{1,5},{5... | collective-permute-start | bytes 3080 | tf_op jit(solution)/shard_map/ppermute | solution.py:16
  18.9 3.6 %collective-permute-start.4 = (s32[256]{0:T(256)S(1)}, s32[256]{0:T(256)S(1)}, u32[]{:S(2)}, u32[]{:S(2)}) collective-permute-start(s32[256]{0:T(256)S(1)} %gather_fusion.4), channel_id=1, source_target_pairs={{0,8},{8,0},{4,12},{12,4},{16,24},{24,16},{20,28},{28,20},{1,9},{9... | collective-permute-start | bytes 3080 | tf_op jit(solution)/shard_map/ppermute | solution.py:16
  24.5 4.5 %collective-permute-start.5 = (s32[256]{0:T(256)S(1)}, s32[256]{0:T(256)S(1)}, u32[]{:S(2)}, u32[]{:S(2)}) collective-permute-start(s32[256]{0:T(256)S(1)} %gather_fusion.5), channel_id=1, source_target_pairs={{0,16},{16,0},{4,20},{20,4},{8,24},{24,8},{12,28},{28,12},{1,17},{... | collective-permute-start | bytes 3080 | tf_op jit(solution)/shard_map/ppermute | solution.py:16
  31.8 6.3 %collective-permute-start.1 = (f32[256,64]{1,0:T(8,128)S(1)}, f32[256,64]{1,0:T(8,128)S(1)}, u32[]{:S(2)}, u32[]{:S(2)}) collective-permute-start(f32[256,64]{1,0:T(8,128)S(1)} %gather_fusion.1), channel_id=1, source_target_pairs={{0,8},{8,0},{4,12},{12,4},{16,24},{24,16},{20,28},{28,20},{1,9},{9... | collective-permute-start | bytes 196616 | tf_op jit(solution)/shard_map/ppermute | solution.py:16
  38.9 10.9 %collective-permute-start.2 = (f32[256,64]{1,0:T(8,128)S(1)}, f32[256,64]{1,0:T(8,128)S(1)}, u32[]{:S(2)}, u32[]{:S(2)}) collective-permute-start(f32[256,64]{1,0:T(8,128)S(1)} %gather_fusion.2), channel_id=1, source_target_pairs={{0,16},{16,0},{4,20},{20,4},{8,24},{24,8},{12,28},{28,12},{1,17},{... | collective-permute-start | bytes 196616 | tf_op jit(solution)/shard_map/ppermute | solution.py:16
  82.2 3.0 copy-start.2
  88.0 191.0 %all-reduce.5.cloned.1.call-start = ((), (), s32[]{:S(2)}) async-start(), calls=%async_computation.1 | async-start | bytes 8388608 | tf_op jit(solution)/shard_map/psum | solution.py:80
  120.2 163.3 %copy-start.1 = (f32[320,256]{1,0:T(8,128)S(1)}, f32[320,256]{1,0:T(8,128)}, u32[]{:S(2)}) copy-start(f32[320,256]{1,0:T(8,128)} %all-reduce.3.cloned.1.call-done) | copy-start | bytes 983044
  279.0 4.5 %copy-start = (f32[256,4096]{1,0:T(8,128)S(1)}, f32[256,4096]{1,0:T(8,128)}, u32[]{:S(2)}) copy-start(f32[256,4096]{1,0:T(8,128)} %all-reduce.5.cloned.1.call-done) | copy-start | bytes 12582916
  283.5 5.4 %slice-start = ((s8[5242880]{0:T(1024)(128)(4,1)}), s8[4194304]{0:T(1024)(128)(4,1)S(1)}, s32[]{:S(2)}) async-start(s8[5242880]{0:T(1024)(128)(4,1)} %bitcast.21), calls=%async_computation.2 | async-start | bytes 8388608
  286.3 2.6 slice-start.1
Sparse Core Ops, SparseCore 0:
  88.2 30.1 all-reduce.2
  122.6 156.3 all-reduce.4
where the time goes:
time: 323 us; the launch traced here: 318 us
  waiting for transfers between devices  196 us (61%)
  matrix products  62.5 us (19%)
  local copies, waits for them, and re-layouts  18.2 us (6%)
  between operations  15.1 us (5%)
  starting transfers between devices  11.8 us (4%)
  other arithmetic  9.13 us (3%)
  blocking collectives  6.24 us (2%)
    psum x1, waiting for transfers between devices, per_device(): pivot_trail = lax.psum(trail[local_rows] * owned, 'row')  159 us
    dot_general x16, matrix products, modmul(): jnp.dot(first_lower, second_lower, preferred_element_type=jnp.float32)  37.5 us
    psum x1, waiting for transfers between devices, per_device(): factors = residue(lax.psum(modmul(panel, inverse_rows), 'col'))  25.4 us
    ppermute x6, starting transfers between devices, swapped(): return lax.ppermute(block, axis, route)  11.7 us
    ppermute x6, waiting for transfers between devices, swapped(): return lax.ppermute(block, axis, route)  11.3 us
    dot_general x16, matrix products, modmul(): jnp.dot(first_upper, second_upper, preferred_element_type=jnp.float32)  9.39 us
    gather x1, local copies, waits for them, and re-layouts, per_device(): pivot_trail = lax.psum(trail[local_rows] * owned, 'row')  8.18 us
    gather x7, local copies, waits for them, and re-layouts, join(): return stacked[picked]  8.1 us
  transfers between devices with their start and end apart: 8, of which 6 were waited for; matrix products, arithmetic and copies ran while one was open for 7% of the time, Pallas kernels for 0%

commit v1 on v0

v1 whole, which is shorter than its diff:
```python
import functools

import jax
import jax.numpy as jnp
from jax import lax
from jax.experimental import pallas as pl
from jax.experimental.pallas import tpu as pltpu
from jax.sharding import PartitionSpec as P

MODULUS = 65521.0
INVERSE = 1.0 / MODULUS
F32 = jnp.float32
BF16 = jnp.bfloat16
I32 = jnp.int32
VMEM = pltpu.MemorySpace.VMEM
SMEM = pltpu.MemorySpace.SMEM
NT = (((1,), (1,)), ((), ()))
TN = (((0,), (0,)), ((), ()))
NN = (((1,), (0,)), ((), ()))


def dot(a, b, dims=NN):
    return lax.dot_general(a, b, dims, preferred_element_type=F32)


def iota(shape, axis):
    return lax.broadcasted_iota(I32, shape, axis)


def ones_where(mask):
    return jnp.where(mask, 1.0, 0.0).astype(BF16)


def high_low(values):
    upper = jnp.floor(values * (1.0 / 256.0))
    return upper.astype(BF16), (values - 256.0 * upper).astype(BF16)


def centred_limbs(values):
    upper = jnp.round(values * (1.0 / 256.0))
    return upper.astype(BF16), (values - 256.0 * upper).astype(BF16)


def centred(values):
    return values - MODULUS * jnp.round(values * INVERSE)


def centred_256(values):
    quotient = jnp.round(values * (256.0 * INVERSE))
    return 256.0 * (values - 256.0 * quotient) + 15.0 * quotient


def left_limbs(values):
    f_upper, f_lower = centred_limbs(values)
    g_upper, g_lower = centred_limbs(centred_256(values))
    upper = jnp.concatenate([g_upper, f_upper], axis=1)
    lower = jnp.concatenate([g_lower, f_lower], axis=1)
    return jnp.concatenate([upper, lower], axis=0)


def right_limbs(values):
    upper, lower = centred_limbs(values)
    return jnp.concatenate([upper, lower], axis=0)


def product(left, right):
    count = left.shape[0]
    both = dot(left_limbs(left), right_limbs(right))
    return centred_256(both[:count]) + both[count:]


def find_kernel(
    devices, first, more, place_ref, node_ref, leaf_ref, panel_ref, trail_ref,
    lower_ref, upper_ref, extra_ref, block_ref, info_ref, most_ref,
    staged, rows, staged_sem, row_sem,
):
    width = node_ref.shape[1]
    row_count = panel_ref.shape[0]
    half = lower_ref.shape[1]
    slots = first + more
    place = place_ref[0]

    nodes = node_ref[...]
    node_upper = nodes >= width
    node_high = ones_where(node_upper)
    node_low = jnp.where(node_upper, nodes - width, nodes).astype(F32).astype(BF16)
    node_index = iota(nodes.shape, 0)
    leaf_high, leaf_low = high_low(leaf_ref[...].astype(F32))

    square = (width, width)
    branch = jnp.zeros((1, width), I32)
    position = iota((1, width), 1)
    for height in reversed(range(devices.bit_length() - 1)):
        offset = devices - (devices >> height)
        hit = ones_where(iota(square, 0) == position)
        chosen = node_index == branch + offset
        high = jnp.sum(jnp.where(chosen, dot(node_high, hit), 0.0), axis=0, keepdims=True)
        low = jnp.sum(jnp.where(chosen, dot(node_low, hit), 0.0), axis=0, keepdims=True)
        branch = 2 * branch + high.astype(I32)
        position = low.astype(I32)
    hit = ones_where(iota(square, 0) == position)
    row_high = dot(leaf_high, hit)
    row_low = dot(leaf_low, hit)

    padded = max(devices, 8)
    owned_by = iota((padded, width), 0) == branch
    earlier = ones_where(iota(square, 0) < iota(square, 1))
    before = dot(ones_where(owned_by), earlier)
    rank = jnp.sum(jnp.where(owned_by, before, 0.0), axis=0, keepdims=True).astype(I32)
    most_ref[0, 0] = jnp.max(rank) + 1
    info_ref[0:1, :] = branch
    info_ref[1:2, :] = rank

    key = jnp.where(branch == place, rank, -1)
    mine = iota((slots, width), 0) == key
    mine_ones = ones_where(mine)
    slot_rows = 256.0 * dot(row_high.astype(BF16), mine_ones, NT) + dot(
        row_low.astype(BF16), mine_ones, NT
    )
    staged[0:1, 0:slots] = jnp.clip(slot_rows.astype(I32), 0, row_count - 1)
    to_scalar = pltpu.make_async_copy(staged, rows, staged_sem)
    to_scalar.start()
    to_scalar.wait()

    def copies(slot):
        row = pl.ds(rows[0, slot], 1)
        if slot < first:
            here = pl.ds(slot, 1)
            return [
                pltpu.make_async_copy(
                    trail_ref.at[row, pl.ds(0, half)], lower_ref.at[here, :], row_sem
                ),
                pltpu.make_async_copy(
                    trail_ref.at[row, pl.ds(half, half)], upper_ref.at[here, :], row_sem
                ),
            ]
        here = pl.ds(slot - first, 1)
        return [
            pltpu.make_async_copy(trail_ref.at[row, :], extra_ref.at[here, :], row_sem)
        ]

    started = [copy for slot in range(slots) for copy in copies(slot)]
    for copy in started:
        copy.start()

    row_values = 256.0 * row_high + row_low
    slot_column = jnp.sum(jnp.where(mine, row_values, 0.0), axis=1, keepdims=True)
    picker = ones_where(iota((slots, row_count), 1) == slot_column.astype(I32))
    panel_high, panel_low = high_low(panel_ref[...])
    block_ref[...] = 256.0 * dot(picker, panel_high) + dot(picker, panel_low)

    for copy in started:
        copy.wait()


def find_pivots(place, node_pick, leaf_pick, panel, trail, devices, first, more):
    width = node_pick.shape[1]
    row_count, part_width = panel.shape
    columns = trail.shape[1]
    half = columns // 2
    lanes = -(-(first + more) // 128) * 128
    whole = pl.BlockSpec(memory_space=VMEM)
    return pl.pallas_call(
        functools.partial(find_kernel, devices, first, more),
        out_shape=(
            jax.ShapeDtypeStruct((first, half), F32),
            jax.ShapeDtypeStruct((first, half), F32),
            jax.ShapeDtypeStruct((more, columns), F32),
            jax.ShapeDtypeStruct((first + more, part_width), F32),
            jax.ShapeDtypeStruct((8, width), I32),
            jax.ShapeDtypeStruct((1, 1), I32),
        ),
        in_specs=[
            pl.BlockSpec(memory_space=SMEM), whole, whole, whole,
            pl.BlockSpec(memory_space=pl.ANY),
        ],
        out_specs=(whole, whole, whole, whole, whole, pl.BlockSpec(memory_space=SMEM)),
        scratch_shapes=[
            pltpu.VMEM((8, lanes), I32),
            pltpu.SMEM((8, lanes), I32),
            pltpu.SemaphoreType.DMA,
            pltpu.SemaphoreType.DMA,
        ],
        compiler_params=pltpu.CompilerParams(vmem_limit_bytes=24 << 20),
        name="find_pivots",
    )(place, node_pick, leaf_pick, panel, trail)


def ring_place(index, devices):
    return jnp.where(index % 2 == 0, index // 2, devices - 1 - index // 2)


def factor_kernel(
    devices, slots, unit, parts, place_ref, info_ref, gathered_ref,
    multiplier_ref, limbs_ref, shift_ref,
):
    width = info_ref.shape[1]
    total = devices * slots
    place = place_ref[0]
    column = place_ref[1]
    owner = info_ref[0:1, :]
    rank = info_ref[1:2, :]

    part_width = width // parts
    source = iota((width, width), 0)
    target = (source // part_width ^ column) * part_width + source % part_width
    reorder = ones_where(target == iota((width, width), 1))
    high, low = high_low(gathered_ref[...])
    high = dot(high, reorder)
    low = dot(low, reorder)

    slot = slots * (owner ^ place) + rank
    picker = ones_where(iota((total, width), 0) == slot)
    block = 256.0 * dot(picker, high[:total].astype(BF16), TN) + dot(
        picker, low[:total].astype(BF16), TN
    )
    panel = centred(256.0 * high[total:] + low[total:])
    diagonal = iota((width, width), 0) == iota((width, width), 1)
    power = centred(block - jnp.where(diagonal, 1.0, 0.0))

    last = (width - 1).bit_length() - 1
    for section in range(last + 1):
        if section < last:
            both = product(jnp.concatenate([power, panel], axis=0), power)
            change = both[width:]
        else:
            change = product(panel, power)
        panel = centred(panel - change if section == 0 else panel + change)
        if section < last:
            power = centred(both[:width])

    multiplier_ref[...] = jnp.where(panel < 0.0, panel + MODULUS, panel) / MODULUS

    shift = centred_256(jnp.sum(panel, axis=1, keepdims=True))
    quotient = jnp.round(shift * (128.0 * INVERSE))
    shift = 128.0 * (shift - 512.0 * quotient) + 15.0 * quotient
    shift_ref[...] = jnp.broadcast_to(shift - 0.5, shift_ref.shape)

    if unit:
        behind = ring_place(place, devices) - ring_place(owner, devices)
        behind = jnp.where(behind < 0, behind + devices, behind)
        arrival = unit * behind + rank
        depth = unit * devices
        twice = jnp.concatenate([arrival, arrival + depth], axis=1)
        order = ones_where(iota((2 * depth, 2 * width), 0) == twice)
        limbs_ref[...] = dot(left_limbs(panel), order, NT).astype(BF16)
    else:
        limbs_ref[...] = left_limbs(panel)


def find_factors(places, info, gathered, devices, slots, unit, parts):
    width = info.shape[1]
    row_count = gathered.shape[0] - devices * slots
    depth = unit * devices if unit else width
    whole = pl.BlockSpec(memory_space=VMEM)
    return pl.pallas_call(
        functools.partial(factor_kernel, devices, slots, unit, parts),
        out_shape=(
            jax.ShapeDtypeStruct((row_count, width), F32),
            jax.ShapeDtypeStruct((2 * row_count, 2 * depth), BF16),
            jax.ShapeDtypeStruct((row_count, 128), F32),
        ),
        in_specs=[pl.BlockSpec(memory_space=SMEM), whole, whole],
        out_specs=(whole, whole, whole),
        compiler_params=pltpu.CompilerParams(vmem_limit_bytes=48 << 20),
        cost_estimate=pl.CostEstimate(
            flops=20_000_000_000, bytes_accessed=4_000_000, transcendentals=0
        ),
        name="find_factors",
    )(places, info, gathered)


def update_kernel(count, limbs_ref, shift_ref, trail_ref, *refs):
    pieces = refs[:count]
    out_ref = refs[-1]
    rows, columns = trail_ref.shape
    values = jnp.concatenate([piece[...] for piece in pieces], axis=0)
    upper = jnp.round(values * (1.0 / 256.0))
    lower = values - 256.0 * upper
    right = jnp.concatenate([(upper - 128.0).astype(BF16), lower.astype(BF16)], axis=0)
    both = dot(limbs_ref[...], right)
    high, low = both[:rows], both[rows:]
    quotient = jnp.round((256.0 * high + low) * INVERSE)
    rest = 256.0 * (high - 256.0 * quotient) + (low + 15.0 * quotient)
    shift = jnp.concatenate([shift_ref[...]] * (columns // 128), axis=1)
    ratio = (trail_ref[...] - shift - rest) * INVERSE
    out_ref[...] = (ratio - 0.5 * INVERSE) - jnp.floor(ratio)


def update(limbs, shift, trail, pieces, first_column, columns, before):
    rows, total = trail.shape
    step = 256
    first = first_column // step
    depth = sum(piece.shape[0] for piece in pieces)

    def fixed(array):
        return pl.BlockSpec(array.shape, lambda i: (0, 0), pipeline_mode=pl.Buffered(1))

    in_specs = [
        fixed(limbs), fixed(shift), pl.BlockSpec((rows, step), lambda i: (0, first + i))
    ]
    in_specs += [pl.BlockSpec((piece.shape[0], step), lambda i: (0, i)) for piece in pieces]
    operands = [limbs, shift, trail, *pieces]
    aliases = {}
    if before is not None:
        in_specs.append(pl.BlockSpec(memory_space=pl.ANY))
        aliases = {len(operands): 0}
        operands.append(before)
    return pl.pallas_call(
        functools.partial(update_kernel, len(pieces)),
        out_shape=jax.ShapeDtypeStruct((rows, total), F32),
        grid=(columns // step,),
        in_specs=in_specs,
        out_specs=pl.BlockSpec((rows, step), lambda i: (0, first + i)),
        input_output_aliases=aliases,
        compiler_params=pltpu.CompilerParams(vmem_limit_bytes=24 << 20),
        cost_estimate=pl.CostEstimate(
            flops=8 * rows * depth * columns,
            bytes_accessed=4 * columns * (2 * rows + depth),
            transcendentals=0,
        ),
        name="update",
    )(*operands)


def swapped(block, axis, bit):
    count = lax.axis_size(axis)
    return lax.ppermute(block, axis, [(place, place ^ 1 << bit) for place in range(count)])


def ring_gather(lower, upper, axis):
    count = lax.axis_size(axis)
    order = list(range(0, count, 2)) + list(range(count - 1, 0, -2))
    ahead = [(order[k], order[(k + 1) % count]) for k in range(count)]
    back = [(there, here) for here, there in ahead]
    found = [{0: lower}, {0: upper}]
    for step in range(1, count // 2 + 1):
        for part in (0, 1):
            held = found[part]
            if step < count // 2 or part == 0:
                held[step] = lax.ppermute(held[step - 1], axis, ahead)
            if step < count // 2 or part == 1:
                source = held[(count - step + 1) % count]
                held[count - step] = lax.ppermute(source, axis, back)
    return [[held[k] for k in range(count)] for held in found]


def per_device(panel, trail, leaf_pick, node_pick):
    width = leaf_pick.shape[1]
    columns = trail.shape[1]
    half = columns // 2
    devices = lax.axis_size("row")
    parts = lax.axis_size("col")
    depth_count = devices.bit_length() - 1
    first = width // devices // 8 * 8 + 8
    more = 8
    place = lax.axis_index("row").astype(I32)
    places = jnp.stack([place, lax.axis_index("col").astype(I32)])
    lower, upper, extra, block, info, most = find_pivots(
        places, node_pick, leaf_pick, panel, trail, devices, first, more
    )

    def gather_panel():
        rows = block
        for bit in range(depth_count):
            rows = jnp.concatenate([rows, swapped(rows, "row", bit)], axis=0)
        both = jnp.concatenate([rows, panel], axis=0)
        for bit in range(parts.bit_length() - 1):
            both = jnp.concatenate([both, swapped(both, "col", bit)], axis=1)
        return both

    def by_ring(unit):
        if unit == first:
            low_unit, high_unit = lower, upper
        else:
            low_unit = jnp.concatenate([lower, extra[:, :half]], axis=0)
            high_unit = jnp.concatenate([upper, extra[:, half:]], axis=0)
        low_units, high_units = ring_gather(low_unit, high_unit, "row")
        multipliers, limbs, shift = find_factors(
            places, info, gather_panel(), devices, first + more, unit, parts
        )
        schur = update(limbs, shift, trail, low_units, 0, half, None)
        schur = update(limbs, shift, trail, high_units, half, half, schur)
        return schur, multipliers

    def in_general():
        owner, rank = info[0], info[1]
        own_rows = jnp.zeros((width,), I32)
        branch, position = jnp.zeros((width,), I32), jnp.arange(width, dtype=I32)
        for height in reversed(range(depth_count)):
            picked = node_pick[devices - (devices >> height) + branch, position]
            branch, position = 2 * branch + picked // width, picked % width
        own_rows = leaf_pick[0][position]
        owned = (owner == place)[:, None]
        rows = jnp.where(owned, trail[own_rows], 0.0)
        wide = jnp.where(owned, panel[own_rows], 0.0)
        for bit in range(depth_count):
            rows = rows + swapped(rows, "row", bit)
            wide = wide + swapped(wide, "row", bit)
        both = jnp.concatenate([wide, panel], axis=0)
        for bit in range(parts.bit_length() - 1):
            both = jnp.concatenate([both, swapped(both, "col", bit)], axis=1)
        natural = jnp.zeros_like(info).at[1].set(jnp.arange(width, dtype=I32))
        natural = natural.at[0].set(place)
        multipliers, limbs, shift = find_factors(
            places, natural, both, 1, width, 0, parts
        )
        schur = update(limbs, shift, trail, [rows], 0, columns, None)
        return schur, multipliers

    level = jnp.where(most[0, 0] <= first, 0, jnp.where(most[0, 0] <= first + more, 1, 2))
    return lax.switch(
        level,
        [functools.partial(by_ring, first), functools.partial(by_ring, first + more), in_general],
    )


def solution(mesh):
    in_specs = (P("row", "col"), P("row", "col"), P("row", None), P())
    out_specs = (P("row", "col"), P("row", None))
    return jax.shard_map(
        per_device, mesh=mesh, in_specs=in_specs, out_specs=out_specs, check_vma=False
    )
```

time: 323 us -> 86.3 us (0.27); the launches traced: 318 us -> 85.9 us
  waiting for transfers between devices: 196 us -> 33.3 us
  matrix products: 62.5 us -> 0 us
  Pallas kernels: 0 us -> 25.4 us
  local copies, waits for them, and re-layouts: 18.2 us -> 1.16 us
  between operations: 15.1 us -> 2 us
  starting transfers between devices: 11.8 us -> 23.4 us
  other arithmetic: 9.13 us -> 0.51 us
  blocking collectives: 6.24 us -> 0 us
    psum x2 -> x0, waiting for transfers between devices: 184 us -> none  [the longest x1 159 us: per_device(): pivot_trail = lax.psum(trail[local_rows] * owned, 'row')]
    dot_general x64 -> x0, matrix products: 62.5 us -> none  [the longest x16 37.5 us: modmul(): jnp.dot(first_lower, second_lower, preferred_element_type=jnp.float32)]
    pallas_call x0 -> x4, Pallas kernels: none -> 25.4 us  [the longest x2 12.1 us: update(): pl.pallas_call(functools.partial(update_kernel, len(pieces)), out_shape=j...]
    ppermute x6 -> x19, waiting for transfers between devices: 11.3 us -> 33.3 us  [the longest x7 12.9 us: ring_gather(): held[step] = lax.ppermute(held[step - 1], axis, ahead)]
    gather x9 -> x0, local copies, waits for them, and re-layouts: 17 us -> none  [the longest x1 8.18 us: per_device(): pivot_trail = lax.psum(trail[local_rows] * owned, 'row')]
    ppermute x6 -> x19, starting transfers between devices: 11.7 us -> 23.4 us  [the longest x7 11.2 us: ring_gather(): held[step] = lax.ppermute(held[step - 1], axis, ahead)]
    all_gather x1 -> x0, blocking collectives: 6.24 us -> none  [per_device(): pivot_block = lax.all_gather(block_part, 'col', axis=1, tiled=True)]
    mul x1 -> x0, other arithmetic: 4.79 us -> none  [per_device(): pivot_trail = lax.psum(trail[local_rows] * owned, 'row')]
  transfers between devices with their start and end apart: 8 -> 19, of which waited for: 6 -> 7; matrix products, arithmetic and copies ran while one was open for 7% -> 1% of each run, Pallas kernels for 0% -> 17%
where the time goes in v1:
time: 86.3 us; the launch traced here: 85.9 us
  waiting for transfers between devices  33.3 us (39%)
  Pallas kernels  25.4 us (29%)
  starting transfers between devices  23.4 us (27%)
  between operations  2 us (2%)
  local copies, waits for them, and re-layouts  1.16 us (1%)
    ppermute x7, waiting for transfers between devices, ring_gather(): held[step] = lax.ppermute(held[step - 1], axis, ahead)  12.9 us
    pallas_call x2, Pallas kernels, update(): pl.pallas_call(functools.partial(update_kernel, len(pieces)), out_shape=j...  12.1 us
    ppermute x7, starting transfers between devices, ring_gather(): held[step] = lax.ppermute(held[step - 1], axis, ahead)  11.2 us
    ppermute x5, waiting for transfers between devices, swapped(): lax.ppermute(block, axis, [(place, place ^ 1 << bit) for place in range(c...  11.1 us
    ppermute x7, waiting for transfers between devices, ring_gather(): held[count - step] = lax.ppermute(source, axis, back)  9.29 us
    ppermute x5, starting transfers between devices, swapped(): lax.ppermute(block, axis, [(place, place ^ 1 << bit) for place in range(c...  9.12 us
    pallas_call x1, Pallas kernels, find_factors(): pl.pallas_call(functools.partial(factor_kernel, devices, slots, unit, par...  8.8 us
    pallas_call x1, Pallas kernels, find_pivots(): pl.pallas_call(functools.partial(find_kernel, devices, first, more), out_...  4.52 us
  transfers between devices with their start and end apart: 19, of which 7 were waited for; matrix products, arithmetic and copies ran while one was open for 1% of the time, Pallas kernels for 17%

profile of v1, /device:TPU:0, one launch (start us, length us, event | category | flops | bytes accessed | tf_op | source)
XLA Modules:
  0.0 85.9 jit_solution(3312637012018159885)
XLA Ops:
  0.7 1.0 %copy.19.panel_ref = f32[320,64]{1,0:T(8,128)S(1)} copy(f32[320,64]{0,1:T(8,128)} %param.11) | data formatting | bytes 163840 | tf_op args[0]
  1.8 4.5 %find_pivots.1 = (f32[40,2048]{1,0:T(8,128)S(1)}, f32[40,2048]{1,0:T(8,128)S(1)}, f32[8,4096]{1,0:T(8,128)S(1)}, f32[48,64]{1,0:T(8,128)S(1)}, s32[8,256]{1,0:T(8,128)S(1)}, /*index=5*/s32[1,1]{1,0:T(1,128)}) custom-call(s32[2]{0:T(128)S(1)} %pad_add_fusion.place_ref, s32[7,256]{1,0:T(8,128)} %node_ref.1, s32[1,256]{1,0:T(1,128)} %leaf_ref.1, ...), custom_call_target="tpu_custom_call" | custom-call | tf_op jit(solution)/shard_map/find_pivots/pallas_call | solution.py:163
  7.6 78.3 %conditional.1 = (f32[320,256]{1,0:T(8,128)}, f32[320,4096]{1,0:T(8,128)}) conditional(s32[]{:T(128)} %bitcast.11, (f32[48,64]{1,0:T(8,128)S(1)}, f32[320,64]{0,1:T(8,128)S(1)}, s32[2]{0:T(128)S(1)}, s32[8,256]{1,0:T(8,128)S(1)}, f32[40,2048]{1,0:T(8,128)S(1)}, /*index=5*/f32[40,2048]{1,0:T(8,128)S(1)}, ...), branch_computations={%region_0.1_spmd, %region_1.2_spmd, %region_2.3_spmd} | conditional | flops 24027209728 | bytes 161772496 | solution.py:412
  7.6 2.9 %collective-permute-start = (f32[48,64]{1,0:T(8,128)S(1)}, f32[48,64]{1,0:T(8,128)S(1)}, u32[]{:S(2)}, u32[]{:S(2)}) collective-permute-start(f32[48,64]{1,0:T(8,128)S(1)} %get-tuple-element.70), channel_id=1, source_target_pairs={{0,4},{4,0},{8,12},{12,8},{16,20},{20,16},{24,28},{28,24},{1,5},{5... | collective-permute-start | bytes 36872 | tf_op jit(solution)/shard_map/cond/branch_0_fun/ppermute | solution.py:328
  10.6 1.5 %collective-permute-start.12 = (f32[40,2048]{1,0:T(8,128)S(1)}, f32[40,2048]{1,0:T(8,128)S(1)}, u32[]{:S(2)}, u32[]{:S(2)}) collective-permute-start(f32[40,2048]{1,0:T(8,128)S(1)} %get-tuple-element.76.refs_0_), channel_id=1, source_target_pairs={{0,8},{8,16},{16,24},{24,28},{28,20},{20,12},{12,4},{4,0},{1,9},{9... | collective-permute-start | bytes 983048 | tf_op jit(solution)/shard_map/cond/branch_0_fun/ppermute | solution.py:341
  12.1 0.5 collective-permute-start.8
  12.7 2.4 %collective-permute-start.1 = (f32[96,64]{1,0:T(8,128)S(1)}, f32[96,64]{1,0:T(8,128)S(1)}, u32[]{:S(2)}, u32[]{:S(2)}) collective-permute-start(f32[96,64]{1,0:T(8,128)S(1)} %pad_maximum_fusion.3), channel_id=1, source_target_pairs={{0,8},{4,12},{8,0},{12,4},{16,24},{20,28},{24,16},{28,20},{1,9},{5... | collective-permute-start | bytes 73736 | tf_op jit(solution)/shard_map/cond/branch_0_fun/ppermute | solution.py:328
  15.1 7.6 %collective-permute-done.1 = f32[96,64]{1,0:T(8,128)S(1)} collective-permute-done((f32[96,64]{1,0:T(8,128)S(1)}, f32[96,64]{1,0:T(8,128)S(1)}, u32[]{:S(2)}, u32[]{:S(2)}) %collective-permute-start.1) | collective-permute-done | bytes 24608 | tf_op jit(solution)/shard_map/cond/branch_0_fun/ppermute | solution.py:328
  22.7 2.1 %collective-permute-start.2 = (f32[192,64]{1,0:T(8,128)S(1)}, f32[192,64]{1,0:T(8,128)S(1)}, u32[]{:S(2)}, u32[]{:S(2)}) collective-permute-start(f32[192,64]{1,0:T(8,128)S(1)} %pad_maximum_fusion.2), channel_id=1, source_target_pairs={{0,16},{4,20},{8,24},{12,28},{16,0},{20,4},{24,8},{28,12},{1,17},{... | collective-permute-start | bytes 147464 | tf_op jit(solution)/shard_map/cond/branch_0_fun/ppermute | solution.py:328
  24.9 3.5 %collective-permute-done.2 = f32[192,64]{1,0:T(8,128)S(1)} collective-permute-done((f32[192,64]{1,0:T(8,128)S(1)}, f32[192,64]{1,0:T(8,128)S(1)}, u32[]{:S(2)}, u32[]{:S(2)}) %collective-permute-start.2) | collective-permute-done | bytes 49184 | tf_op jit(solution)/shard_map/cond/branch_0_fun/ppermute | solution.py:328
  28.5 0.3 collective-permute-start.16
  28.8 1.8 %collective-permute-start.5 = (f32[40,2048]{1,0:T(8,128)S(1)}, f32[40,2048]{1,0:T(8,128)S(1)}, u32[]{:S(2)}, u32[]{:S(2)}) collective-permute-start(f32[40,2048]{1,0:T(8,128)S(1)} %get-tuple-element.75.refs_0_), channel_id=1, source_target_pairs={{0,8},{8,16},{16,24},{24,28},{28,20},{20,12},{12,4},{4,0},{1,9},{9... | collective-permute-start | bytes 983048 | tf_op jit(solution)/shard_map/cond/branch_0_fun/ppermute | solution.py:341
  30.6 0.6 collective-permute-start.13
  31.2 1.5 %collective-permute-start.9 = (f32[40,2048]{1,0:T(8,128)S(1)}, f32[40,2048]{1,0:T(8,128)S(1)}, u32[]{:S(2)}, u32[]{:S(2)}) collective-permute-start(f32[40,2048]{1,0:T(8,128)S(1)} %collective-permute-done.8.refs_7_), channel_id=1, source_target_pairs={{8,0},{16,8},{24,16},{28,24},{20,28},{12,20},{4,12},{0,4},{9,1},{1... | collective-permute-start | bytes 983048 | tf_op jit(solution)/shard_map/cond/branch_0_fun/ppermute | solution.py:344
  32.8 1.6 %collective-permute-start.4 = (f32[704,128]{1,0:T(8,128)S(1)}, f32[704,128]{1,0:T(8,128)S(1)}, u32[]{:S(2)}, u32[]{:S(2)}) collective-permute-start(f32[704,128]{1,0:T(8,128)S(1)} %pad_maximum_fusion.1), channel_id=1, source_target_pairs={{0,2},{1,3},{2,0},{3,1},{4,6},{5,7},{6,4},{7,5},{8,10},{9,11},{10,... | collective-permute-start | bytes 1081352 | tf_op jit(solution)/shard_map/cond/branch_0_fun/ppermute | solution.py:328
  34.4 4.8 %collective-permute-done.16.refs_7_ = f32[40,2048]{1,0:T(8,128)S(1)} collective-permute-done((f32[40,2048]{1,0:T(8,128)S(1)}, f32[40,2048]{1,0:T(8,128)S(1)}, u32[]{:S(2)}, u32[]{:S(2)}) %collective-permute-start.16) | collective-permute-done | bytes 327712 | tf_op jit(solution)/shard_map/cond/branch_0_fun/ppermute | solution.py:344
  39.1 0.2 collective-permute-start.17
  39.4 1.8 %collective-permute-start.6 = (f32[40,2048]{1,0:T(8,128)S(1)}, f32[40,2048]{1,0:T(8,128)S(1)}, u32[]{:S(2)}, u32[]{:S(2)}) collective-permute-start(f32[40,2048]{1,0:T(8,128)S(1)} %collective-permute-done.5.refs_1_), channel_id=1, source_target_pairs={{0,8},{8,16},{16,24},{24,28},{28,20},{20,12},{12,4},{4,0},{1,9},{9... | collective-permute-start | bytes 983048 | tf_op jit(solution)/shard_map/cond/branch_0_fun/ppermute | solution.py:341
  41.2 5.2 %collective-permute-done.13.refs_2_ = f32[40,2048]{1,0:T(8,128)S(1)} collective-permute-done((f32[40,2048]{1,0:T(8,128)S(1)}, f32[40,2048]{1,0:T(8,128)S(1)}, u32[]{:S(2)}, u32[]{:S(2)}) %collective-permute-start.13) | collective-permute-done | bytes 327712 | tf_op jit(solution)/shard_map/cond/branch_0_fun/ppermute | solution.py:341
  46.4 1.8 %collective-permute-start.14 = (f32[40,2048]{1,0:T(8,128)S(1)}, f32[40,2048]{1,0:T(8,128)S(1)}, u32[]{:S(2)}, u32[]{:S(2)}) collective-permute-start(f32[40,2048]{1,0:T(8,128)S(1)} %collective-permute-done.13.refs_2_), channel_id=1, source_target_pairs={{0,8},{8,16},{16,24},{24,28},{28,20},{20,12},{12,4},{4,0},{1,9},{9... | collective-permute-start | bytes 983048 | tf_op jit(solution)/shard_map/cond/branch_0_fun/ppermute | solution.py:341
  48.2 0.2 collective-permute-start.10
  48.4 0.3 pad_maximum_fusion.gathered_ref
  48.7 4.5 %collective-permute-done.17.refs_6_ = f32[40,2048]{1,0:T(8,128)S(1)} collective-permute-done((f32[40,2048]{1,0:T(8,128)S(1)}, f32[40,2048]{1,0:T(8,128)S(1)}, u32[]{:S(2)}, u32[]{:S(2)}) %collective-permute-start.17) | collective-permute-done | bytes 327712 | tf_op jit(solution)/shard_map/cond/branch_0_fun/ppermute | solution.py:344
  53.2 0.2 collective-permute-start.18
  53.4 1.8 %collective-permute-start.7 = (f32[40,2048]{1,0:T(8,128)S(1)}, f32[40,2048]{1,0:T(8,128)S(1)}, u32[]{:S(2)}, u32[]{:S(2)}) collective-permute-start(f32[40,2048]{1,0:T(8,128)S(1)} %collective-permute-done.6.refs_2_), channel_id=1, source_target_pairs={{0,8},{8,16},{16,24},{24,28},{28,20},{20,12},{12,4},{4,0},{1,9},{9... | collective-permute-start | bytes 983048 | tf_op jit(solution)/shard_map/cond/branch_0_fun/ppermute | solution.py:341
  55.2 5.2 %collective-permute-done.14.refs_3_ = f32[40,2048]{1,0:T(8,128)S(1)} collective-permute-done((f32[40,2048]{1,0:T(8,128)S(1)}, f32[40,2048]{1,0:T(8,128)S(1)}, u32[]{:S(2)}, u32[]{:S(2)}) %collective-permute-start.14) | collective-permute-done | bytes 327712 | tf_op jit(solution)/shard_map/cond/branch_0_fun/ppermute | solution.py:341
  60.4 1.8 %collective-permute-start.15 = (f32[40,2048]{1,0:T(8,128)S(1)}, f32[40,2048]{1,0:T(8,128)S(1)}, u32[]{:S(2)}, u32[]{:S(2)}) collective-permute-start(f32[40,2048]{1,0:T(8,128)S(1)} %collective-permute-done.14.refs_3_), channel_id=1, source_target_pairs={{0,8},{8,16},{16,24},{24,28},{28,20},{20,12},{12,4},{4,0},{1,9},{9... | collective-permute-start | bytes 983048 | tf_op jit(solution)/shard_map/cond/branch_0_fun/ppermute | solution.py:341
  62.2 0.2 collective-permute-start.11
  62.5 8.8 %find_factors.3 = (f32[320,256]{1,0:T(8,128)}, bf16[640,640]{1,0:T(8,128)(2,1)S(1)}, f32[320,128]{1,0:T(8,128)S(1)}) custom-call(s32[2]{0:T(128)S(1)} %get-tuple-element.68.place_ref, s32[8,256]{1,0:T(8,128)S(1)} %get-tuple-element.69.info_ref, f32[704,256]{1,0:T(8,128)S(1)} %pad_maximum_fusion.gathered_ref), custom_call_target="tpu_custom_call" | custom-call | flops 20000000000 | bytes 4000000 | tf_op jit(solution)/shard_map/cond/branch_0_fun/find_factors/pallas_call | solution.py:256
  71.3 2.5 %collective-permute-done.15.refs_4_ = f32[40,2048]{1,0:T(8,128)S(1)} collective-permute-done((f32[40,2048]{1,0:T(8,128)S(1)}, f32[40,2048]{1,0:T(8,128)S(1)}, u32[]{:S(2)}, u32[]{:S(2)}) %collective-permute-start.15) | collective-permute-done | bytes 327712 | tf_op jit(solution)/shard_map/cond/branch_0_fun/ppermute | solution.py:341
  73.7 6.0 %update.5.refs_8_ = f32[320,4096]{1,0:T(8,128)} custom-call(bf16[640,640]{1,0:T(8,128)(2,1)S(1)} %get-tuple-element.72.limbs_ref, f32[320,128]{1,0:T(8,128)S(1)} %get-tuple-element.73.shift_ref, f32[320,4096]{1,0:T(8,128)S(1)} %bitcast.14, f32[40,2048]{1,0:T(8,128)S(1)} %get-tuple-element.76.refs_0_, f32[40,2048]{1,0:T(8,128)S(1)} %collective-permute-done.12.refs_1_, ...), custom_call_target="tpu_custom_call" | custom-call | flops 1677721600 | bytes 7864320 | tf_op jit(solution)/shard_map/cond/branch_0_fun/update/pallas_call | solution.py:309
  79.8 6.1 %update.6 = f32[320,4096]{1,0:T(8,128)} custom-call(bf16[640,640]{1,0:T(8,128)(2,1)S(1)} %get-tuple-element.72.limbs_ref, f32[320,128]{1,0:T(8,128)S(1)} %get-tuple-element.73.shift_ref, f32[320,4096]{1,0:T(8,128)S(1)} %bitcast.14, f32[40,2048]{1,0:T(8,128)S(1)} %get-tuple-element.75.refs_0_, ...), custom_call_target="tpu_custom_call", output_to_operand_aliasing={{}: (11, {})} | custom-call | flops 1677721600 | bytes 7864320 | tf_op jit(solution)/shard_map/cond/branch_0_fun/update/pallas_call | solution.py:309
  (34 shorter events, 0.5 us)
Async XLA Ops:
  0.6 7.0 %copy-start.3 = (f32[320,64]{0,1:T(8,128)S(1)}, f32[320,64]{0,1:T(8,128)}, u32[]{:S(2)}) copy-start(f32[320,64]{0,1:T(8,128)} %param.11) | copy-start | bytes 245764
  0.6 7.0 %copy-start = (s32[7,256]{1,0:T(8,128)S(1)}, s32[7,256]{1,0:T(8,128)}, u32[]{:S(2)}) copy-start(s32[7,256]{1,0:T(8,128)} %node_ref.1) | copy-start | bytes 21508
  0.7 6.9 %copy-start.1 = (s32[1,256]{1,0:T(1,128)S(1)}, s32[1,256]{1,0:T(1,128)}, u32[]{:S(2)}) copy-start(s32[1,256]{1,0:T(1,128)} %leaf_ref.1) | copy-start | bytes 3076
  7.6 5.1 %collective-permute-start = (f32[48,64]{1,0:T(8,128)S(1)}, f32[48,64]{1,0:T(8,128)S(1)}, u32[]{:S(2)}, u32[]{:S(2)}) collective-permute-start(f32[48,64]{1,0:T(8,128)S(1)} %get-tuple-element.70), channel_id=1, source_target_pairs={{0,4},{4,0},{8,12},{12,8},{16,20},{20,16},{24,28},{28,24},{1,5},{5... | collective-permute-start | bytes 36872 | tf_op jit(solution)/shard_map/cond/branch_0_fun/ppermute | solution.py:328
  10.6 20.0 %collective-permute-start.12 = (f32[40,2048]{1,0:T(8,128)S(1)}, f32[40,2048]{1,0:T(8,128)S(1)}, u32[]{:S(2)}, u32[]{:S(2)}) collective-permute-start(f32[40,2048]{1,0:T(8,128)S(1)} %get-tuple-element.76.refs_0_), channel_id=1, source_target_pairs={{0,8},{8,16},{16,24},{24,28},{28,20},{20,12},{12,4},{4,0},{1,9},{9... | collective-permute-start | bytes 983048 | tf_op jit(solution)/shard_map/cond/branch_0_fun/ppermute | solution.py:341
  12.1 19.1 %collective-permute-start.8 = (f32[40,2048]{1,0:T(8,128)S(1)}, f32[40,2048]{1,0:T(8,128)S(1)}, u32[]{:S(2)}, u32[]{:S(2)}) collective-permute-start(f32[40,2048]{1,0:T(8,128)S(1)} %get-tuple-element.75.refs_0_), channel_id=1, source_target_pairs={{8,0},{16,8},{24,16},{28,24},{20,28},{12,20},{4,12},{0,4},{9,1},{1... | collective-permute-start | bytes 983048 | tf_op jit(solution)/shard_map/cond/branch_0_fun/ppermute | solution.py:344
  12.7 10.0 %collective-permute-start.1 = (f32[96,64]{1,0:T(8,128)S(1)}, f32[96,64]{1,0:T(8,128)S(1)}, u32[]{:S(2)}, u32[]{:S(2)}) collective-permute-start(f32[96,64]{1,0:T(8,128)S(1)} %pad_maximum_fusion.3), channel_id=1, source_target_pairs={{0,8},{4,12},{8,0},{12,4},{16,24},{20,28},{24,16},{28,20},{1,9},{5... | collective-permute-start | bytes 73736 | tf_op jit(solution)/shard_map/cond/branch_0_fun/ppermute | solution.py:328
  22.7 5.7 %collective-permute-start.2 = (f32[192,64]{1,0:T(8,128)S(1)}, f32[192,64]{1,0:T(8,128)S(1)}, u32[]{:S(2)}, u32[]{:S(2)}) collective-permute-start(f32[192,64]{1,0:T(8,128)S(1)} %pad_maximum_fusion.2), channel_id=1, source_target_pairs={{0,16},{4,20},{8,24},{12,28},{16,0},{20,4},{24,8},{28,12},{1,17},{... | collective-permute-start | bytes 147464 | tf_op jit(solution)/shard_map/cond/branch_0_fun/ppermute | solution.py:328
  28.4 4.2 %collective-permute-start.3 = (f32[704,64]{1,0:T(8,128)S(1)}, f32[704,64]{1,0:T(8,128)S(1)}, u32[]{:S(2)}, u32[]{:S(2)}) collective-permute-start(f32[704,64]{1,0:T(8,128)S(1)} %constant_dynamic-update-slice_fusion), channel_id=1, source_target_pairs={{0,1},{1,0},{2,3},{3,2},{4,5},{5,4},{6,7},{7,6},{8,9},{9,8},{10,11... | collective-permute-start | bytes 540680 | tf_op jit(solution)/shard_map/cond/branch_0_fun/ppermute | solution.py:328
  28.5 10.6 %collective-permute-start.16 = (f32[40,2048]{1,0:T(8,128)S(1)}, f32[40,2048]{1,0:T(8,128)S(1)}, u32[]{:S(2)}, u32[]{:S(2)}) collective-permute-start(f32[40,2048]{1,0:T(8,128)S(1)} %get-tuple-element.76.refs_0_), channel_id=1, source_target_pairs={{8,0},{16,8},{24,16},{28,24},{20,28},{12,20},{4,12},{0,4},{9,1},{1... | collective-permute-start | bytes 983048 | tf_op jit(solution)/shard_map/cond/branch_0_fun/ppermute | solution.py:344
  28.8 10.6 %collective-permute-start.5 = (f32[40,2048]{1,0:T(8,128)S(1)}, f32[40,2048]{1,0:T(8,128)S(1)}, u32[]{:S(2)}, u32[]{:S(2)}) collective-permute-start(f32[40,2048]{1,0:T(8,128)S(1)} %get-tuple-element.75.refs_0_), channel_id=1, source_target_pairs={{0,8},{8,16},{16,24},{24,28},{28,20},{20,12},{12,4},{4,0},{1,9},{9... | collective-permute-start | bytes 983048 | tf_op jit(solution)/shard_map/cond/branch_0_fun/ppermute | solution.py:341
  30.6 15.8 %collective-permute-start.13 = (f32[40,2048]{1,0:T(8,128)S(1)}, f32[40,2048]{1,0:T(8,128)S(1)}, u32[]{:S(2)}, u32[]{:S(2)}) collective-permute-start(f32[40,2048]{1,0:T(8,128)S(1)} %collective-permute-done.12.refs_1_), channel_id=1, source_target_pairs={{0,8},{8,16},{16,24},{24,28},{28,20},{20,12},{12,4},{4,0},{1,9},{9... | collective-permute-start | bytes 983048 | tf_op jit(solution)/shard_map/cond/branch_0_fun/ppermute | solution.py:341
  31.2 17.0 %collective-permute-start.9 = (f32[40,2048]{1,0:T(8,128)S(1)}, f32[40,2048]{1,0:T(8,128)S(1)}, u32[]{:S(2)}, u32[]{:S(2)}) collective-permute-start(f32[40,2048]{1,0:T(8,128)S(1)} %collective-permute-done.8.refs_7_), channel_id=1, source_target_pairs={{8,0},{16,8},{24,16},{28,24},{20,28},{12,20},{4,12},{0,4},{9,1},{1... | collective-permute-start | bytes 983048 | tf_op jit(solution)/shard_map/cond/branch_0_fun/ppermute | solution.py:344
  32.8 15.6 %collective-permute-start.4 = (f32[704,128]{1,0:T(8,128)S(1)}, f32[704,128]{1,0:T(8,128)S(1)}, u32[]{:S(2)}, u32[]{:S(2)}) collective-permute-start(f32[704,128]{1,0:T(8,128)S(1)} %pad_maximum_fusion.1), channel_id=1, source_target_pairs={{0,2},{1,3},{2,0},{3,1},{4,6},{5,7},{6,4},{7,5},{8,10},{9,11},{10,... | collective-permute-start | bytes 1081352 | tf_op jit(solution)/shard_map/cond/branch_0_fun/ppermute | solution.py:328
  39.1 14.0 %collective-permute-start.17 = (f32[40,2048]{1,0:T(8,128)S(1)}, f32[40,2048]{1,0:T(8,128)S(1)}, u32[]{:S(2)}, u32[]{:S(2)}) collective-permute-start(f32[40,2048]{1,0:T(8,128)S(1)} %collective-permute-done.16.refs_7_), channel_id=1, source_target_pairs={{8,0},{16,8},{24,16},{28,24},{20,28},{12,20},{4,12},{0,4},{9,1},{1... | collective-permute-start | bytes 983048 | tf_op jit(solution)/shard_map/cond/branch_0_fun/ppermute | solution.py:344
  39.4 14.0 %collective-permute-start.6 = (f32[40,2048]{1,0:T(8,128)S(1)}, f32[40,2048]{1,0:T(8,128)S(1)}, u32[]{:S(2)}, u32[]{:S(2)}) collective-permute-start(f32[40,2048]{1,0:T(8,128)S(1)} %collective-permute-done.5.refs_1_), channel_id=1, source_target_pairs={{0,8},{8,16},{16,24},{24,28},{28,20},{20,12},{12,4},{4,0},{1,9},{9... | collective-permute-start | bytes 983048 | tf_op jit(solution)/shard_map/cond/branch_0_fun/ppermute | solution.py:341
  46.4 14.0 %collective-permute-start.14 = (f32[40,2048]{1,0:T(8,128)S(1)}, f32[40,2048]{1,0:T(8,128)S(1)}, u32[]{:S(2)}, u32[]{:S(2)}) collective-permute-start(f32[40,2048]{1,0:T(8,128)S(1)} %collective-permute-done.13.refs_2_), channel_id=1, source_target_pairs={{0,8},{8,16},{16,24},{24,28},{28,20},{20,12},{12,4},{4,0},{1,9},{9... | collective-permute-start | bytes 983048 | tf_op jit(solution)/shard_map/cond/branch_0_fun/ppermute | solution.py:341
  48.2 14.0 %collective-permute-start.10 = (f32[40,2048]{1,0:T(8,128)S(1)}, f32[40,2048]{1,0:T(8,128)S(1)}, u32[]{:S(2)}, u32[]{:S(2)}) collective-permute-start(f32[40,2048]{1,0:T(8,128)S(1)} %collective-permute-done.9.refs_6_), channel_id=1, source_target_pairs={{8,0},{16,8},{24,16},{28,24},{20,28},{12,20},{4,12},{0,4},{9,1},{1... | collective-permute-start | bytes 983048 | tf_op jit(solution)/shard_map/cond/branch_0_fun/ppermute | solution.py:344
  48.4 25.3 %slice-start = ((s8[5242880]{0:T(1024)(128)(4,1)}), s8[4194304]{0:T(1024)(128)(4,1)S(1)}, s32[]{:S(2)}) async-start(s8[5242880]{0:T(1024)(128)(4,1)} %bitcast.13), calls=%async_computation | async-start | bytes 8388608 | tf_op jit(solution)/shard_map/cond
  53.2 18.1 %collective-permute-start.18 = (f32[40,2048]{1,0:T(8,128)S(1)}, f32[40,2048]{1,0:T(8,128)S(1)}, u32[]{:S(2)}, u32[]{:S(2)}) collective-permute-start(f32[40,2048]{1,0:T(8,128)S(1)} %collective-permute-done.17.refs_6_), channel_id=1, source_target_pairs={{8,0},{16,8},{24,16},{28,24},{20,28},{12,20},{4,12},{0,4},{9,1},{1... | collective-permute-start | bytes 983048 | tf_op jit(solution)/shard_map/cond/branch_0_fun/ppermute | solution.py:344
  53.4 26.4 %collective-permute-start.7 = (f32[40,2048]{1,0:T(8,128)S(1)}, f32[40,2048]{1,0:T(8,128)S(1)}, u32[]{:S(2)}, u32[]{:S(2)}) collective-permute-start(f32[40,2048]{1,0:T(8,128)S(1)} %collective-permute-done.6.refs_2_), channel_id=1, source_target_pairs={{0,8},{8,16},{16,24},{24,28},{28,20},{20,12},{12,4},{4,0},{1,9},{9... | collective-permute-start | bytes 983048 | tf_op jit(solution)/shard_map/cond/branch_0_fun/ppermute | solution.py:341
  60.4 13.3 %collective-permute-start.15 = (f32[40,2048]{1,0:T(8,128)S(1)}, f32[40,2048]{1,0:T(8,128)S(1)}, u32[]{:S(2)}, u32[]{:S(2)}) collective-permute-start(f32[40,2048]{1,0:T(8,128)S(1)} %collective-permute-done.14.refs_3_), channel_id=1, source_target_pairs={{0,8},{8,16},{16,24},{24,28},{28,20},{20,12},{12,4},{4,0},{1,9},{9... | collective-permute-start | bytes 983048 | tf_op jit(solution)/shard_map/cond/branch_0_fun/ppermute | solution.py:341
  62.2 17.6 %collective-permute-start.11 = (f32[40,2048]{1,0:T(8,128)S(1)}, f32[40,2048]{1,0:T(8,128)S(1)}, u32[]{:S(2)}, u32[]{:S(2)}) collective-permute-start(f32[40,2048]{1,0:T(8,128)S(1)} %collective-permute-done.10.refs_5_), channel_id=1, source_target_pairs={{8,0},{16,8},{24,16},{28,24},{20,28},{12,20},{4,12},{0,4},{9,1},{1... | collective-permute-start | bytes 983048 | tf_op jit(solution)/shard_map/cond/branch_0_fun/ppermute | solution.py:344
  62.5 11.3 %slice-start.1 = ((s8[5242880]{0:T(1024)(128)(4,1)}), s8[1048576]{0:T(1024)(128)(4,1)S(1)}, s32[]{:S(2)}) async-start(s8[5242880]{0:T(1024)(128)(4,1)} %bitcast.13), calls=%async_computation.1 | async-start | bytes 2097152 | tf_op jit(solution)/shard_map/cond
